TPU v7x, 32 devices: a whole 2x2x4 slice. The times are simulated.
32 devices in a mesh: row: 4 (over z), col: 8 (over y, x, core).
Axes of the slice: x: 2, y: 2, z: 4, core: 2. Of those that a mesh axis runs over, the one named last changes fastest.
Arguments:
- ancestor_pivot: float32 [8, 512, 4, 1024], P(None, 'row', None, 'col'), as said below
- child_pivot: float32 [8, 512, 4, 1024], P(None, 'row', None, 'col'), as said below
- child_panel: float32 [8, 512, 4, 1024], P(None, 'row', None, 'col'), may hold values from -0.09375 to 0.09375
- block_pattern: int32 [32, 32], replicated, may hold values 0 or 1
Outputs:
- child_inverse: float32 [8, 512, 4, 1024], P(None, 'row', None, 'col')
Inputs may be any that keep to these rules, and one draw needn't show every extreme that they name: ancestor_pivot is an exactly symmetric 4096 x 4096 matrix. child_pivot is an exactly symmetric 4096 x 4096 matrix.
All inputs are finite; a program needn't handle non-finite values.
Results may differ from a plain program's by a relative error of at most 0.00005.
Values sent between devices are 32-bit elements; how exact they have to be, the bound alone decides.
A program may use at most 128 MiB of HBM per device.

v0:
```python
import jax
import jax.numpy as jnp
from jax import lax
from jax.sharding import PartitionSpec as P


def column_term(stationary, local_rows, piece):
    shaped = piece.reshape(local_rows, piece.shape[2], piece.shape[3])
    return jnp.einsum(
        "kcl,kn->cln",
        shaped,
        stationary,
        precision=lax.Precision.HIGHEST,
        preferred_element_type=jnp.float32,
    )


def local(ancestor_pivot, child_pivot, child_panel, block_pattern):
    anc_blocks = child_panel.shape[0]
    block_size = child_panel.shape[1]
    col_blocks = child_panel.shape[2]
    anc_col_blocks = ancestor_pivot.shape[2]
    child_rows = child_pivot.shape[0]
    row_count = lax.axis_size("row")
    col_count = lax.axis_size("col")
    row_index = lax.axis_index("row")
    col_index = lax.axis_index("col")
    local_rows = anc_blocks * block_size
    local_cols = col_blocks * block_size
    blocks = block_pattern.reshape(anc_blocks, row_count, col_blocks, col_count)
    local_mask = lax.dynamic_index_in_dim(blocks, row_index, 1, keepdims=False)
    local_mask = lax.dynamic_index_in_dim(local_mask, col_index, 2, keepdims=False)
    masked = child_panel * local_mask.astype(jnp.float32)[:, None, :, None]
    masked_flat = masked.reshape(local_rows, local_cols)
    panel_all = lax.all_gather(masked, "row", axis=1, tiled=True)
    panel_split = panel_all.reshape(anc_col_blocks, col_count * block_size, local_cols)
    segment = lax.all_gather(ancestor_pivot, "col", axis=3, tiled=True)
    length = segment.shape[3]
    weights = segment.reshape(local_rows, anc_col_blocks, length)
    product = jnp.einsum(
        "kcl,cln->kn",
        weights,
        panel_split,
        precision=lax.Precision.HIGHEST,
        preferred_element_type=jnp.float32,
    )
    product_blocks = product.reshape(anc_blocks, block_size, col_blocks, block_size)
    term = column_term(
        masked_flat, local_rows, lax.all_gather(product_blocks, "col", axis=3, tiled=True)
    )
    term = term.reshape(child_rows, row_count, block_size, local_cols)
    term = jnp.transpose(term, (1, 0, 2, 3)).reshape(
        row_count * child_rows * block_size, local_cols
    )
    summed = lax.psum_scatter(term, "row", scatter_dimension=0, tiled=True)
    return child_pivot + summed.reshape(child_rows, block_size, col_blocks, block_size)


def solution(mesh):
    return jax.shard_map(
        local,
        mesh=mesh,
        in_specs=(
            P(None, "row", None, "col"),
            P(None, "row", None, "col"),
            P(None, "row", None, "col"),
            P(),
        ),
        out_specs=P(None, "row", None, "col"),
        check_vma=False,
    )
```

profile of v0, /device:TPU:0, one launch (start us, length us, event | category | flops | bytes accessed | tf_op | source)
XLA Modules:
  0.0 626.5 jit_solution(12353932388971323393)
XLA Ops:
  6.5 0.0 all-gather.4.cloned.1.call-start
  6.5 0.8 reshape.28
  7.4 0.1 constant_dynamic-slice_fusion
  7.4 0.1 copy.15
  7.6 0.1 copy.9
  7.6 3.4 broadcast_multiply_fusion
  11.0 0.0 all-gather.4.cloned.1.call-update
  11.0 0.0 all-gather.6.cloned.1.call-start
  11.1 0.7 all-gather.6.cloned.1.call-update
  11.8 0.0 all-gather.8.cloned.1.call-start
  11.8 151.7 %all-gather.4.cloned.1.call-done = f32[8,512,4,128]{3,2,1,0:T(4,128)} async-done(((f32[8,128,4,128]{3,2,1,0:T(4,128)}), f32[8,512,4,128]{3,2,1,0:T(4,128)}) %all-gather.4.cloned.1.call-update) | async-done | bytes 8388624 | tf_op jit(solution)/shard_map/all_gather | solution.py:35
  163.5 10.5 %reshape.29 = f32[4,1024,512]{2,1,0:T(8,128)} reshape(f32[8,512,4,128]{3,2,1,0:T(4,128)} %all-gather.4.cloned.1.call-done) | data formatting | bytes 16777216 | tf_op jit(solution)/shard_map/reshape | solution.py:36
  174.0 82.6 %all-gather.6.cloned.1.call-done = f32[8,128,4,1024]{3,2,1,0:T(4,128)} async-done(((f32[8,128,4,128]{3,2,1,0:T(4,128)}), f32[8,128,4,1024]{3,2,1,0:T(4,128)}) %all-gather.6.cloned.1.call-update) | async-done | bytes 16777232 | tf_op jit(solution)/shard_map/all_gather | solution.py:37
  256.6 0.0 copy-start.1
  256.6 15.3 %copy.10 = f32[8,128,4,1024]{3,1,0,2:T(8,128)S(1)} copy(f32[8,128,4,1024]{3,2,1,0:T(4,128)} %all-gather.6.cloned.1.call-done) | data formatting | bytes 33554432 | tf_op jit(solution)/shard_map/all_gather | solution.py:37
  272.0 0.0 copy-done.1
  272.0 0.0 copy-start
  272.0 54.8 %convolution_bitcast_fusion.1 = f32[64,8,8,128]{3,1,2,0:T(8,128)S(1)} fusion(f32[4,1024,512]{2,1,0:T(8,128)S(1)} %copy-done.1, f32[1024,4,1024]{2,0,1:T(8,128)S(1)} %bitcast.29), kind=kOutput, calls=%fused_computation.2 | convolution fusion | flops 25769803776 | bytes 27262976 | tf_op jit(solution)/shard_map/kcl,cln->kn/dot_general | solution.py:40
  326.9 1.8 copy.16
  328.6 0.0 all-gather.8.cloned.1.call-update
  328.7 0.0 reduce-scatter.2.cloned.1.call-start
  328.7 0.0 copy-done
  328.7 1.8 reshape.37
  330.6 88.0 %all-gather.8.cloned.1.call-done = f32[8,128,4,1024]{1,0,3,2:T(8,128)} async-done(((f32[8,128,4,128]{1,0,3,2:T(8,128)}), f32[8,128,4,1024]{1,0,3,2:T(8,128)}) %all-gather.8.cloned.1.call-update) | async-done | bytes 16777232 | tf_op jit(solution)/shard_map/all_gather | solution.py:49
  418.5 18.0 %reshape.32 = f32[1024,4,1024]{0,2,1:T(8,128)} reshape(f32[8,128,4,1024]{1,0,3,2:T(8,128)} %all-gather.8.cloned.1.call-done) | data formatting | bytes 33554432 | tf_op jit(solution)/shard_map/reshape | solution.py:8
  436.5 0.0 copy-done.2
  436.5 29.1 %convolution_bitcast_fusion = f32[4,8,128,512]{3,2,0,1:T(8,128)S(1)} fusion(f32[8,4,128,1024]{3,2,1,0:T(8,128)} %bitcast.30, f32[1024,512,1,1]{1,0,2,3:T(8,128)S(1)} %copy-done.2), kind=kOutput, calls=%fused_computation | convolution fusion | flops 25769803776 | bytes 27262976 | tf_op jit(solution)/shard_map/kcl,kn->cln/dot_general | solution.py:9
  465.6 4.2 copy.12
  469.8 0.0 reduce-scatter.2.cloned.1.call-update
  469.9 144.8 %reduce-scatter.2.cloned.1.call-done = f32[1024,512]{1,0:T(8,128)} async-done(((f32[4096,512]{1,0:T(8,128)}), f32[1024,512]{1,0:T(8,128)}) %reduce-scatter.2.cloned.1.call-update) | async-done | bytes 2097168 | tf_op jit(solution)/shard_map/reduce_scatter | solution.py:55
  614.6 1.9 reshape.35
  616.6 3.5 add.19
  (2 shorter events, 0.0 us)
Async XLA Ops:
  6.5 157.0 %all-gather.4.cloned.1.call-start = ((), (), s32[]{:S(2)}) async-start(), calls=%async_computation.1 | async-start | bytes 10485760 | tf_op jit(solution)/shard_map/all_gather | solution.py:35
  11.0 245.6 %all-gather.6.cloned.1.call-start = ((), (), s32[]{:S(2)}) async-start(), calls=%async_computation.2 | async-start | bytes 18874368 | tf_op jit(solution)/shard_map/all_gather | solution.py:37
  11.8 406.8 %all-gather.8.cloned.1.call-start = ((), (), s32[]{:S(2)}) async-start(), calls=%async_computation.3 | async-start | bytes 18874368 | tf_op jit(solution)/shard_map/all_gather | solution.py:49
  256.6 15.4 %copy-start.1 = (f32[4,1024,512]{2,1,0:T(8,128)S(1)}, f32[4,1024,512]{2,1,0:T(8,128)}, u32[]{:S(2)}) copy-start(f32[4,1024,512]{2,1,0:T(8,128)} %reshape.29) | copy-start | bytes 25165828
  272.0 56.7 %copy-start = (f32[8,128,4,128]{3,2,1,0:T(4,128)S(1)}, f32[8,128,4,128]{3,2,1,0:T(4,128)}, u32[]{:S(2)}) copy-start(f32[8,128,4,128]{3,2,1,0:T(4,128)} %broadcast_multiply_fusion) | copy-start | bytes 6291460
  328.7 286.0 %reduce-scatter.2.cloned.1.call-start = ((), (), s32[]{:S(2)}) async-start(), calls=%async_computation.4 | async-start | bytes 10485760 | tf_op jit(solution)/shard_map/reduce_scatter | solution.py:55
  330.6 106.0 %copy-start.2 = (f32[1024,512,1,1]{1,0,2,3:T(8,128)S(1)}, f32[1024,512,1,1]{1,0,2,3:T(8,128)}, u32[]{:S(2)}) copy-start(f32[1024,512,1,1]{1,0,2,3:T(8,128)} %reshape.37) | copy-start | bytes 6291460
Sparse Core Ops, SparseCore 0:
  11.1 152.3 all-gather.3
  165.4 91.1 all-gather.5
  328.8 89.7 all-gather.7
  470.0 144.6 reduce-scatter.1
where the time goes:
time: 627 us
  waiting for transfers between devices  468 us (75%)
  matrix products  83.9 us (13%)
  local copies, waits for them, and re-layouts  54.7 us (9%)
  between operations  13.2 us (2%)
  other arithmetic  6.82 us (1%)
    all_gather x1, waiting for transfers between devices, local(): panel_all = lax.all_gather(masked, 'row', axis=1, tiled=True)  152 us
    reduce_scatter x1, waiting for transfers between devices, local(): summed = lax.psum_scatter(term, 'row', scatter_dimension=0, tiled=True)  145 us
    all_gather x1, waiting for transfers between devices, local(): lax.all_gather(product_blocks, 'col', axis=3, tiled=True)  88 us
    all_gather x1, waiting for transfers between devices, local(): segment = lax.all_gather(ancestor_pivot, 'col', axis=3, tiled=True)  82.6 us
    dot_general x1, matrix products, local(): jnp.einsum('kcl,cln->kn', weights, panel_split, precision=lax.Precision.H...  54.8 us
    dot_general x1, matrix products, column_term(): jnp.einsum('kcl,kn->cln', shaped, stationary, precision=lax.Precision.HIG...  29.1 us
    reshape x1, local copies, waits for them, and re-layouts, column_term(): shaped = piece.reshape(local_rows, piece.shape[2], piece.shape[3])  18 us
    all_gather x1, local copies, waits for them, and re-layouts, local(): segment = lax.all_gather(ancestor_pivot, 'col', axis=3, tiled=True)  15.3 us
  transfers between devices with their start and end apart: 4, of which 4 were waited for; matrix products, arithmetic and copies ran while one was open for 2% of the time, Pallas kernels for 0%

commit v1 on v0

v1 whole, which is shorter than its diff:
```python
import functools

import jax
import jax.numpy as jnp
from jax import lax
from jax.experimental import pallas as pl
from jax.experimental.pallas import tpu as pltpu
from jax.sharding import PartitionSpec as P

MESH = pl.DeviceIdType.MESH


def flip(index, mask):
    bit = 1
    while bit <= mask:
        if mask & bit:
            index = index + bit - 2 * bit * ((index // bit) % 2)
        bit *= 2
    return index


def halves_of(x):
    high = x.astype(jnp.bfloat16)
    return high, (x - high.astype(jnp.float32)).astype(jnp.bfloat16)


def dot3(a, b, dims):
    a_high, a_low = a
    b_high, b_low = b
    dot = functools.partial(
        lax.dot_general, dimension_numbers=(dims, ((), ())), preferred_element_type=jnp.float32
    )
    return dot(a_low, b_high) + dot(a_high, b_low) + dot(a_high, b_high)


def kernel(
    n_row, n_col, a_in, m_in, out, pieces, panel, slots, term, w_high, w_low, b_high, b_low,
    local_sem, col_send, col_recv, row_send, row_recv, sum_send, sum_recv,
):
    r = lax.axis_index("row")
    c = lax.axis_index("col")
    rows, cols = a_in.shape
    ratio = n_col // n_row
    half = rows // 2
    tile = min(rows, 256)
    strip = min(cols, 256)
    high_bits = [1 << i for i in range(1, n_col.bit_length() - 1)]
    orders = (high_bits + [1], high_bits[::-1] + [1])
    stages = len(orders[0])

    def col_copy(which, part, mask, bit):
        place = pieces.at[which, flip(c, mask), pl.ds(part * half, half)]
        return pltpu.make_async_remote_copy(
            src_ref=place,
            dst_ref=place,
            send_sem=col_send.at[which, part, mask ^ bit],
            recv_sem=col_recv.at[which, part, mask],
            device_id={"col": flip(c, bit)},
            device_id_type=MESH,
        )

    def col_send_piece(which, part, mask, bit):
        place = pieces.at[which, flip(c, mask), pl.ds(part * half, half)]
        pltpu.make_async_remote_copy(
            src_ref=place,
            dst_ref=place,
            send_sem=col_send.at[which, part, mask ^ bit],
            recv_sem=col_recv.at[which, part, mask ^ bit],
            device_id={"col": flip(c, bit)},
            device_id_type=MESH,
        ).start()

    def col_start(which):
        for s in range(stages):
            for part in range(2):
                col_send_piece(which, part, 0, orders[part][s])

    def col_stage(which, s):
        for part in range(2):
            order = orders[part]
            held = [0]
            for bit in order[:s]:
                held = held + [m ^ bit for m in held]
            for m in held:
                mask = m ^ order[s]
                col_copy(which, part, mask, order[s]).wait_recv()
                for bit in order[s + 1:]:
                    col_send_piece(which, part, mask, bit)

    def col_finish(which):
        for part in range(2):
            for mask in range(1, n_col):
                pltpu.make_async_remote_copy(
                    src_ref=pieces.at[which, c, pl.ds(part * half, half)],
                    dst_ref=pieces.at[which, c, pl.ds(part * half, half)],
                    send_sem=col_send.at[which, part, mask],
                    recv_sem=col_recv.at[which, part, mask],
                    device_id={"col": flip(c, 1)},
                    device_id_type=MESH,
                ).wait_send()

    def row_copy(d, block, step):
        return pltpu.make_async_remote_copy(
            src_ref=panel.at[block],
            dst_ref=panel.at[block],
            send_sem=row_send.at[d, step],
            recv_sem=row_recv.at[d, step],
            device_id={"row": (r + 1 - 2 * d + n_row) % n_row},
            device_id_type=MESH,
        )

    def sends(d, step):
        block = r - (step - 1) * (1 - 2 * d)
        there = r + 1 - 2 * d
        return block, (block >= 0) & (block < n_row) & (there >= 0) & (there < n_row)

    def receives(d, step):
        block = r - step * (1 - 2 * d)
        return block, (block >= 0) & (block < n_row)

    def row_start(step):
        for d in range(2):
            block, yes = sends(d, step)

            @pl.when(yes)
            def _():
                row_copy(d, block, step).start()

    def row_wait(step):
        for d in range(2):
            block, yes = receives(d, step)

            @pl.when(yes)
            def _():
                row_copy(d, block, step).wait_recv()

    def first_product(block):
        @pl.loop(0, ratio)
        def _(g):
            high, low = halves_of(panel[block, pl.ds(pl.multiple_of(g * cols, cols), cols), :])
            w_high[...] = high
            w_low[...] = low

            @pl.loop(0, rows // tile)
            def _(i):
                at = pl.ds(pl.multiple_of(i * tile, tile), tile)
                a = halves_of(pieces[0, block + g * n_row, at, :])
                out[at, :] += dot3(a, (w_high[...], w_low[...]), ((1,), (0,)))

    def first_products(step):
        @pl.loop(0, 2)
        def _(d):
            block, yes = receives(d, step)

            @pl.when(yes)
            def _():
                first_product(block)

    def second_product(block, g):
        @pl.loop(0, cols // strip)
        def _(i):
            at = pl.ds(pl.multiple_of(i * strip, strip), strip)
            m = halves_of(pieces[1, block + g * n_row, :, at])
            term[at, :] = dot3(m, (b_high[...], b_low[...]), ((0,), (0,)))

    def sum_copy(place, there_place, g, there):
        at = pl.ds(pl.multiple_of(g * cols, cols), cols)
        return pltpu.make_async_remote_copy(
            src_ref=slots.at[place, at],
            dst_ref=slots.at[there_place, at],
            send_sem=sum_send.at[place, g],
            recv_sem=sum_recv.at[there_place, g],
            device_id={"row": there},
            device_id_type=MESH,
        )

    copies = [
        pltpu.make_async_copy(a_in, pieces.at[0, c], local_sem.at[0]),
        pltpu.make_async_copy(m_in, panel.at[r], local_sem.at[1]),
        pltpu.make_async_copy(m_in, pieces.at[1, c], local_sem.at[2]),
    ]
    for copy in copies:
        copy.start()
    barrier = pltpu.get_barrier_semaphore()
    for bit in orders[0]:
        pl.semaphore_signal(barrier, inc=1, device_id={"col": flip(c, bit)}, device_id_type=MESH)
    for hop in (1, n_row - 1):
        pl.semaphore_signal(
            barrier, inc=1, device_id={"row": (r + hop) % n_row}, device_id_type=MESH
        )
    pl.semaphore_wait(barrier, stages + 2)
    for copy in copies:
        copy.wait()
    row_start(1)
    col_start(0)
    out[...] = jnp.zeros_like(out)
    col_stage(0, 0)
    row_wait(1)
    if n_row > 2:
        row_start(2)
    col_start(1)
    for s in range(1, stages):
        col_stage(0, s)
    first_product(r)
    for step in range(2, n_row):
        row_wait(step)
        if step + 1 < n_row:
            row_start(step + 1)
        if step == 2:
            col_stage(1, 0)
            first_products(1)
        if step + 1 == n_row:
            for s in range(1, stages - 1):
                col_stage(1, s)
        first_products(step)
    high, low = halves_of(out[...])
    b_high[...] = high
    b_low[...] = low
    col_stage(1, stages - 1)

    swap = (2 * r) // n_row

    def decode(index):
        u = index // (2 * ratio)
        g = (index // 2) % ratio
        d = (index + swap) % 2
        block = d * u + (1 - d) * (n_row - 1 - u)
        return g, d, block, (block - r) * (1 - 2 * d) > 0

    @pl.loop(0, (n_row - 1) * ratio * 2)
    def _(index):
        g, d, block, yes = decode(index)

        @pl.when(yes)
        def _():
            second_product(block, g)
            at = pl.ds(pl.multiple_of(g * cols, cols), cols)
            there = r + 1 - 2 * d
            fed = r * (1 - d) + (n_row - 1 - r) * d

            @pl.when(fed > 0)
            def _():
                sum_copy(block, block, g, there).wait_recv()
                slots[block, at, :] += term[...]

            @pl.when(fed <= 0)
            def _():
                slots[block, at, :] = term[...]

            last = jnp.where(block == there, d, 0)
            sum_copy(block, block + last * (n_row - block), g, there).start()

    beside = jnp.where(r > 0, r - 1, r + 1)

    @pl.loop(0, ratio)
    def _(g):
        at = pl.ds(pl.multiple_of(g * cols, cols), cols)
        second_product(r, g)
        out[at, :] = term[...]

        @pl.when(r > 0)
        def _():
            sum_copy(r, r, g, beside).wait_recv()
            out[at, :] += slots[r, at, :]

        @pl.when(r < n_row - 1)
        def _():
            sum_copy(r, n_row, g, beside).wait_recv()
            out[at, :] += slots[n_row, at, :]

    for which in range(2):
        col_finish(which)
    for step in range(1, n_row):
        for d in range(2):
            block, yes = sends(d, step)

            @pl.when(yes)
            def _():
                row_copy(d, block, step).wait_send()

    @pl.loop(0, (n_row - 1) * ratio * 2)
    def _(index):
        g, d, block, yes = decode(index)

        @pl.when(yes)
        def _():
            sum_copy(block, block, g, r + 1 - 2 * d).wait_send()


def local(n_row, n_col, ancestor_pivot, child_pivot, child_panel, block_pattern):
    blocks, size, col_blocks, width = child_panel.shape
    ratio = n_col // n_row
    rows, cols = blocks * size, col_blocks * width
    split = (col_blocks, ratio, size, cols)
    mask = block_pattern.reshape(blocks, n_row, col_blocks, n_col)
    mask = lax.dynamic_index_in_dim(mask, lax.axis_index("row"), 1, keepdims=False)
    mask = lax.dynamic_index_in_dim(mask, lax.axis_index("col"), 2, keepdims=False)
    masked = child_panel * mask.astype(jnp.float32)[:, None, :, None]

    def ordered(x):
        return jnp.transpose(x.reshape(split), (1, 0, 2, 3)).reshape(rows, cols)

    summed = pl.pallas_call(
        functools.partial(kernel, n_row, n_col),
        out_shape=jax.ShapeDtypeStruct((rows, cols), jnp.float32),
        in_specs=[pl.BlockSpec(memory_space=pl.ANY)] * 2,
        out_specs=pl.BlockSpec(memory_space=pltpu.VMEM),
        scratch_shapes=[
            pltpu.VMEM((2, n_col, rows, cols), jnp.float32),
            pltpu.VMEM((n_row, rows, cols), jnp.float32),
            pltpu.VMEM((n_row + 1, rows, cols), jnp.float32),
            pltpu.VMEM((cols, cols), jnp.float32),
            pltpu.VMEM((cols, cols), jnp.bfloat16),
            pltpu.VMEM((cols, cols), jnp.bfloat16),
            pltpu.VMEM((rows, cols), jnp.bfloat16),
            pltpu.VMEM((rows, cols), jnp.bfloat16),
            pltpu.SemaphoreType.DMA((3,)),
            pltpu.SemaphoreType.DMA((2, 2, n_col)),
            pltpu.SemaphoreType.DMA((2, 2, n_col)),
            pltpu.SemaphoreType.DMA((2, n_row)),
            pltpu.SemaphoreType.DMA((2, n_row)),
            pltpu.SemaphoreType.DMA((n_row + 1, ratio)),
            pltpu.SemaphoreType.DMA((n_row + 1, ratio)),
        ],
        compiler_params=pltpu.CompilerParams(
            collective_id=0, has_side_effects=True, vmem_limit_bytes=67043328
        ),
    )(ordered(ancestor_pivot), ordered(masked))
    back = jnp.transpose(summed.reshape(ratio, col_blocks, size, cols), (1, 0, 2, 3))
    return child_pivot + back.reshape(child_pivot.shape)


def solution(mesh):
    spec = P(None, "row", None, "col")
    return jax.shard_map(
        functools.partial(local, mesh.shape["row"], mesh.shape["col"]),
        mesh=mesh,
        in_specs=(spec, spec, spec, P()),
        out_specs=spec,
        check_vma=False,
    )
```

time: 627 us -> 310 us (0.49)
  waiting for transfers between devices: 468 us -> 0 us
  Pallas kernels: 0 us -> 288 us
  matrix products: 83.9 us -> 0 us
  local copies, waits for them, and re-layouts: 54.7 us -> 14.7 us
  between operations: 13.2 us -> 0.04 us
    all_gather x3 -> x0, waiting for transfers between devices: 322 us -> none  [the longest x1 152 us: local(): panel_all = lax.all_gather(masked, 'row', axis=1, tiled=True)]
    pallas_call x0 -> x1, Pallas kernels: none -> 288 us  [local(): pl.pallas_call(functools.partial(kernel, n_row, n_col), out_shape=jax.Sha...]
    reduce_scatter x1 -> x0, waiting for transfers between devices: 145 us -> none  [local(): summed = lax.psum_scatter(term, 'row', scatter_dimension=0, tiled=True)]
    dot_general x2 -> x0, matrix products: 83.9 us -> none  [the longest x1 54.8 us: local(): jnp.einsum('kcl,cln->kn', weights, panel_split, precision=lax.Precision.H...]
    reshape x5 -> x6, local copies, waits for them, and re-layouts: 33.1 us -> 11.4 us  [the longest x4 8.65 us: ordered(): return jnp.transpose(x.reshape(split), (1, 0, 2, 3)).reshape(rows, cols)]
    all_gather x1 -> x0, local copies, waits for them, and re-layouts: 15.3 us -> none  [local(): segment = lax.all_gather(ancestor_pivot, 'col', axis=3, tiled=True)]
  transfers between devices with their start and end apart: 4 -> 0, of which waited for: 4 -> 0; matrix products, arithmetic and copies ran while one was open for 2% -> 0% of each run, Pallas kernels for 0% -> 0%
where the time goes in v1:
time: 310 us; the launch traced here: 309 us
  Pallas kernels  288 us (93%)
  local copies, waits for them, and re-layouts  14.7 us (5%)
  other arithmetic  5.49 us (2%)
    pallas_call x1, Pallas kernels, local(): pl.pallas_call(functools.partial(kernel, n_row, n_col), out_shape=jax.Sha...  288 us
    reshape x4, local copies, waits for them, and re-layouts, ordered(): return jnp.transpose(x.reshape(split), (1, 0, 2, 3)).reshape(rows, cols)  8.65 us

profile of v1, /device:TPU:0, one launch (start us, length us, event | category | flops | bytes accessed | tf_op | source)
XLA Modules:
  0.0 308.7 jit_solution(17808017821216114171)
XLA Ops:
  0.0 0.8 reshape.25
  0.8 0.1 constant_dynamic-slice_fusion
  0.9 0.1 copy.10
  1.0 0.1 copy.7
  1.1 2.0 broadcast_multiply_fusion
  3.1 1.8 reshape.26
  5.0 3.1 %copy.8 = f32[4,2,128,512]{3,2,0,1:T(8,128)} copy(f32[4,2,128,512]{3,2,1,0:T(8,128)} %reshape.26) | data formatting | bytes 4194304 | tf_op jit(solution)/shard_map/reshape | solution.py:301
  8.1 2.1 reshape.23
  10.2 1.6 copy.5
  11.8 288.4 %shard_map.46 = f32[1024,512]{1,0:T(8,128)} custom-call(f32[1024,512]{1,0:T(8,128)} %bitcast.14, f32[1024,512]{1,0:T(8,128)} %bitcast.13), custom_call_target="tpu_custom_call" | custom-call | tf_op jit(solution)/shard_map/pallas_call | solution.py:303
  300.2 3.1 copy.9
  303.3 1.9 reshape.29
  305.2 3.5 %add.17 = f32[8,128,4,128]{3,2,1,0:T(4,128)} add(f32[8,128,4,128]{3,2,1,0:T(4,128)} %param.5, f32[8,128,4,128]{3,2,1,0:T(4,128)S(1)} %reshape.29) | non-fusion elementwise | flops 524288 | bytes 6291456 | tf_op jit(solution)/shard_map/add | solution.py:330
  (1 shorter events, 0.0 us)

commit v2 on v1

--- a/solution.py
+++ b/solution.py
@@ -34,13 +34,14 @@
 
 
 def kernel(
-    n_row, n_col, a_in, m_in, out, pieces, panel, slots, term, w_high, w_low, b_high, b_low,
+    n_row, n_col, size, a_in, m_in, out, pieces, panel, slots, term, w_high, w_low, b_high, b_low,
     local_sem, col_send, col_recv, row_send, row_recv, sum_send, sum_recv,
 ):
     r = lax.axis_index("row")
     c = lax.axis_index("col")
     rows, cols = a_in.shape
     ratio = n_col // n_row
+    blocks = rows // size
     half = rows // 2
     tile = min(rows, 256)
     strip = min(cols, 256)
@@ -174,11 +175,15 @@
             device_id_type=MESH,
         )
 
-    copies = [
-        pltpu.make_async_copy(a_in, pieces.at[0, c], local_sem.at[0]),
-        pltpu.make_async_copy(m_in, panel.at[r], local_sem.at[1]),
-        pltpu.make_async_copy(m_in, pieces.at[1, c], local_sem.at[2]),
-    ]
+    copies = []
+    for i in range(blocks):
+        came = pl.ds(i * size, size)
+        goes = pl.ds(((i % ratio) * (blocks // ratio) + i // ratio) * size, size)
+        copies += [
+            pltpu.make_async_copy(a_in.at[came], pieces.at[0, c, goes], local_sem.at[0, i]),
+            pltpu.make_async_copy(m_in.at[came], panel.at[r, goes], local_sem.at[1, i]),
+            pltpu.make_async_copy(m_in.at[came], pieces.at[1, c, goes], local_sem.at[2, i]),
+        ]
     for copy in copies:
         copy.start()
     barrier = pltpu.get_barrier_semaphore()
@@ -256,17 +261,20 @@
     def _(g):
         at = pl.ds(pl.multiple_of(g * cols, cols), cols)
         second_product(r, g)
-        out[at, :] = term[...]
 
         @pl.when(r > 0)
         def _():
             sum_copy(r, r, g, beside).wait_recv()
-            out[at, :] += slots[r, at, :]
+            term[...] += slots[r, at, :]
 
         @pl.when(r < n_row - 1)
         def _():
             sum_copy(r, n_row, g, beside).wait_recv()
-            out[at, :] += slots[n_row, at, :]
+            term[...] += slots[n_row, at, :]
+
+        for j in range(blocks // ratio):
+            to = pl.ds(pl.multiple_of((ratio * j + g) * size, size), size)
+            out[to, :] = term[pl.ds(j * size, size), :]
 
     for which in range(2):
         col_finish(which)
@@ -291,17 +299,13 @@
     blocks, size, col_blocks, width = child_panel.shape
     ratio = n_col // n_row
     rows, cols = blocks * size, col_blocks * width
-    split = (col_blocks, ratio, size, cols)
     mask = block_pattern.reshape(blocks, n_row, col_blocks, n_col)
     mask = lax.dynamic_index_in_dim(mask, lax.axis_index("row"), 1, keepdims=False)
     mask = lax.dynamic_index_in_dim(mask, lax.axis_index("col"), 2, keepdims=False)
     masked = child_panel * mask.astype(jnp.float32)[:, None, :, None]
 
-    def ordered(x):
-        return jnp.transpose(x.reshape(split), (1, 0, 2, 3)).reshape(rows, cols)
-
     summed = pl.pallas_call(
-        functools.partial(kernel, n_row, n_col),
+        functools.partial(kernel, n_row, n_col, size),
         out_shape=jax.ShapeDtypeStruct((rows, cols), jnp.float32),
         in_specs=[pl.BlockSpec(memory_space=pl.ANY)] * 2,
         out_specs=pl.BlockSpec(memory_space=pltpu.VMEM),
@@ -314,7 +318,7 @@
             pltpu.VMEM((cols, cols), jnp.bfloat16),
             pltpu.VMEM((rows, cols), jnp.bfloat16),
             pltpu.VMEM((rows, cols), jnp.bfloat16),
-            pltpu.SemaphoreType.DMA((3,)),
+            pltpu.SemaphoreType.DMA((3, blocks)),
             pltpu.SemaphoreType.DMA((2, 2, n_col)),
             pltpu.SemaphoreType.DMA((2, 2, n_col)),
             pltpu.SemaphoreType.DMA((2, n_row)),
@@ -325,9 +329,8 @@
         compiler_params=pltpu.CompilerParams(
             collective_id=0, has_side_effects=True, vmem_limit_bytes=67043328
         ),
-    )(ordered(ancestor_pivot), ordered(masked))
-    back = jnp.transpose(summed.reshape(ratio, col_blocks, size, cols), (1, 0, 2, 3))
-    return child_pivot + back.reshape(child_pivot.shape)
+    )(ancestor_pivot.reshape(rows, cols), masked.reshape(rows, cols))
+    return child_pivot + summed.reshape(child_pivot.shape)
 
 
 def solution(mesh):

time: 310 us -> 301 us (0.971)
  local copies, waits for them, and re-layouts: 14.7 us -> 5.52 us
    reshape x5 -> x2, local copies, waits for them, and re-layouts: 10.6 us -> 4.41 us  [the longest x1 2.47 us: local(): masked.reshape(rows, cols)]
where the time goes in v2:
time: 301 us; the launch traced here: 300 us
  Pallas kernels  289 us (96%)
  other arithmetic  5.64 us (2%)
  local copies, waits for them, and re-layouts  5.52 us (2%)
    pallas_call x1, Pallas kernels, local(): pl.pallas_call(functools.partial(kernel, n_row, n_col, size), out_shape=j...  289 us

profile of v2, /device:TPU:0, one launch (start us, length us, event | category | flops | bytes accessed | tf_op | source)
XLA Modules:
  0.0 299.8 jit_solution(4641716677895788047)
XLA Ops:
  0.0 0.8 reshape.15
  0.8 0.1 constant_dynamic-slice_fusion
  0.9 0.1 copy.7
  1.0 0.1 copy.6
  1.1 0.0 copy-start
  1.1 2.2 broadcast_multiply_fusion
  3.3 0.0 copy-done
  3.3 2.5 copy_bitcast_fusion
  5.8 288.6 %shard_map.46 = f32[1024,512]{1,0:T(8,128)} custom-call(f32[1024,512]{1,0:T(8,128)} %get-tuple-element.6.a_in, f32[1024,512]{1,0:T(8,128)} %get-tuple-element.5.m_in), custom_call_target="tpu_custom_call" | custom-call | tf_op jit(solution)/shard_map/pallas_call | solution.py:307
  294.4 1.9 reshape.17
  296.4 3.5 %add.17 = f32[8,128,4,128]{3,2,1,0:T(4,128)} add(f32[8,128,4,128]{3,2,1,0:T(4,128)} %param.5, f32[8,128,4,128]{3,2,1,0:T(4,128)S(1)} %reshape.17) | non-fusion elementwise | flops 524288 | bytes 6291456 | tf_op jit(solution)/shard_map/add | solution.py:333
  (1 shorter events, 0.0 us)
Async XLA Ops:
  1.1 2.2 copy-start
